TPU v7x, 32 devices: a whole 2x2x4 slice. The times are simulated.
32 devices in a mesh: wide: 16 (over z, y, x), narrow: 2 (over core).
Axes of the slice: x: 2, y: 2, z: 4, core: 2. Of those that a mesh axis runs over, the one named last changes fastest.
Arguments:
- positions: float32 [3, 8192], P(None, ('wide', 'narrow')), may hold values from 0 to 1
- forces: float32 [3, 16, 8192], P(None, None, ('wide', 'narrow')), may hold values from -6 to 6
- waves: int32 [3, 8192], replicated, may hold values from -16 to 16, as said below
Outputs:
- velocity: float32 [3, 16, 8192], P(None, None, ('wide', 'narrow'))
Inputs may be any that keep to these rules, and one draw needn't show every extreme that they name: `waves`: no wavevector is (0, 0, 0).
All inputs are finite; a program needn't handle non-finite values.
Results may differ from a plain program's by a relative error of at most 0.0053.
Values may be sent and summed in bfloat16 or wider, within the bound.
No kernel may reach another device: no remote copies, remote signals or barrier semaphores. Data moves between devices by JAX's collectives and lax.ppermute only.
A program may use at most 64 MiB of HBM per device.

v0:
```python
import jax
import jax.numpy as jnp
from jax import lax
from jax.sharding import PartitionSpec as P

two_pi = 6.283185307179586
radius = 0.005
xi_split = 40.0


def make_tables(wblock, positions):
    mf = wblock.astype(jnp.float32)
    theta = two_pi * (
        mf[0][:, None] * positions[0][None, :]
        + mf[1][:, None] * positions[1][None, :]
        + mf[2][:, None] * positions[2][None, :]
    )
    return (jnp.cos(theta).astype(jnp.bfloat16), jnp.sin(theta).astype(jnp.bfloat16))


def scale_sums(sums, wblock, amp):
    cols = sums.shape[1]
    split = sums.reshape(2, 3, -1, cols)
    kvec = two_pi * wblock.astype(jnp.float32)
    ksq = jnp.sum(kvec * kvec, axis=0)
    inner = jnp.sum(kvec[None, :, None, :] * split, axis=1)
    proj = split - kvec[None, :, None, :] * (inner / ksq)[:, None, :, :]
    qarg = ksq / (4.0 * xi_split * xi_split)
    factor = (
        amp
        * (1.0 - radius * radius * ksq / 3.0)
        * (1.0 + qarg + 2.0 * qarg * qarg)
        * jnp.exp(-qarg)
        / ksq
    )
    return (proj * factor).reshape(sums.shape[0], cols).astype(jnp.bfloat16)


def shards(positions, forces, waves):
    rows = positions.shape[1]
    kwaves = waves.shape[1]
    devices = lax.axis_size("wide") * lax.axis_size("narrow")
    force_bf = forces.reshape(-1, rows).astype(jnp.bfloat16)
    half = force_bf.shape[0]
    width = 256
    dims = (((1,), (1,)), ((), ()))
    cos_table, sin_table = make_tables(waves, positions)
    sum_cos = lax.dot_general(force_bf, cos_table, dims, preferred_element_type=jnp.float32)
    sum_sin = lax.dot_general(force_bf, sin_table, dims, preferred_element_type=jnp.float32)
    terms = jnp.concatenate([sum_cos, sum_sin], axis=0)
    amp = 20000.0 / jnp.sqrt(jnp.float32(rows * devices) * jnp.float32(kwaves))

    def apply_block(total, piece, begin, cols):
        cosine = lax.dynamic_slice_in_dim(cos_table, begin, cols, 0)
        sine = lax.dynamic_slice_in_dim(sin_table, begin, cols, 0)
        total = total + jnp.dot(piece[:half], cosine, preferred_element_type=jnp.float32)
        return total + jnp.dot(piece[half:], sine, preferred_element_type=jnp.float32)

    empty = jnp.zeros((half, rows), jnp.float32)
    owned = lax.psum_scatter(terms, ("wide", "narrow"), scatter_dimension=1, tiled=True)
    cols = owned.shape[1]
    wblock = lax.dynamic_slice_in_dim(waves, lax.axis_index(("wide", "narrow")) * cols, cols, 1)
    scaled = scale_sums(owned, wblock, amp)
    piece = lax.all_gather(scaled, ("wide", "narrow"), axis=1, tiled=True)
    cols = piece.shape[1]

    def inner(step, acc):
        sub = lax.dynamic_slice_in_dim(piece, step * width, width, 1)
        return apply_block(acc, sub, step * width, width)

    total = lax.fori_loop(0, cols // width, inner, empty)
    return total.reshape(forces.shape)


def solution(mesh):
    placed = (P(None, ("wide", "narrow")), P(None, None, ("wide", "narrow")), P())
    return jax.shard_map(
        shards,
        mesh=mesh,
        in_specs=placed,
        out_specs=P(None, None, ("wide", "narrow")),
        check_vma=False,
    )
```

profile of v0, /device:TPU:0, one launch (start us, length us, event | category | flops | bytes accessed | tf_op | source)
XLA Modules:
  0.0 309.1 jit_solution(3159215597644270184)
XLA Ops:
  9.2 29.7 %convolution_bitcast_fusion.1 = f32[48,8192]{1,0:T(8,128)S(1)} fusion(bf16[48,256]{1,0:T(8,128)(2,1)S(1)} %bitcast.35, f32[256]{0:T(256)S(1)} %bitcast.40, f32[8192]{0:T(1024)S(1)} %bitcast.29, f32[256]{0:T(256)S(1)} %bitcast.43, f32[8192]{0:T(1024)S(1)} %bitcast.32, f32[256]{0:T(256)S(1)} %bitcast.37, f32[8192]{0:T(1024)S(1)} %bitcast.26), kind=kOutput, calls=%fused_computation.9 | convolution fusion | flops 216006656 | bytes 1698816 | tf_op jit(solution)/shard_map/dot_general | solution.py:48
  38.9 30.4 %convolution_bitcast_fusion = f32[48,8192]{1,0:T(8,128)S(1)} fusion(bf16[48,256]{1,0:T(8,128)(2,1)S(1)} %bitcast.36, f32[256]{0:T(256)S(1)} %bitcast.41, f32[8192]{0:T(1024)S(1)} %bitcast.30, f32[256]{0:T(256)S(1)} %bitcast.44, f32[8192]{0:T(1024)S(1)} %bitcast.33, f32[256]{0:T(256)S(1)} %bitcast.38, f32[8192]{0:T(1024)S(1)} %bitcast.27), kind=kOutput, calls=%fused_computation.8 | convolution fusion | flops 216006656 | bytes 1698816 | tf_op jit(solution)/shard_map/dot_general | solution.py:49
  69.3 1.9 pad_maximum_fusion
  72.0 104.2 %reduce-scatter.2.cloned.1.call-done = f32[96,256]{1,0:T(8,128)} async-done(((f32[96,8192]{1,0:T(8,128)}), f32[96,256]{1,0:T(8,128)}) %reduce-scatter.2.cloned.1.call-update) | async-done | bytes 98320 | tf_op jit(solution)/shard_map/reduce_scatter | solution.py:60
  177.1 1.5 fusion.7
  178.7 34.2 %sine_convert_fusion = (bf16[8192,256]{1,0:T(8,128)(2,1)}, bf16[8192,256]{1,0:T(8,128)(2,1)}) fusion(f32[256]{0:T(256)S(1)} %bitcast.42, f32[8192]{0:T(1024)S(1)} %bitcast.31, f32[256]{0:T(256)S(1)} %bitcast.45, f32[8192]{0:T(1024)S(1)} %bitcast.34, f32[256]{0:T(256)S(1)} %bitcast.39, f32[8192]{0:T(1024)S(1)} %bitcast.28), kind=kLoop, calls=%fused_computation.10 | loop fusion | flops 16777216 | bytes 8489984 | tf_op jit(solution)/shard_map/convert_element_type | solution.py:18
  212.9 19.7 %all-gather.2.cloned.1.call-done = bf16[96,8192]{1,0:T(8,128)(2,1)} async-done(((bf16[96,256]{1,0:T(8,128)(2,1)}), bf16[96,8192]{1,0:T(8,128)(2,1)}) %all-gather.2.cloned.1.call-update) | async-done | bytes 1572880 | tf_op jit(solution)/shard_map/all_gather | solution.py:64
  232.6 69.0 %while.14 = (s32[]{:T(128)}, f32[48,256]{1,0:T(8,128)S(1)}, bf16[96,8192]{1,0:T(8,128)(2,1)}, bf16[8192,256]{1,0:T(8,128)(2,1)}, bf16[8192,256]{1,0:T(8,128)(2,1...) while((s32[]{:T(128)}, f32[48,256]{1,0:T(8,128)S(1)}, bf16[96,8192]{1,0:T(8,128)(2,1)}, ...), condition=%wide.region_4.0_spmd.clone, body=%wide.region_3.0_spmd.clone.sunk | while | flops 12619784 | bytes 511144 | solution.py:71
  233.7 1.1 convolution_add_fusion.5
  234.8 1.1 convolution_add_fusion.4
  235.8 1.1 convolution_add_fusion.5
  236.9 1.1 convolution_add_fusion.4
  238.0 1.1 convolution_add_fusion.5
  239.1 1.1 convolution_add_fusion.4
  240.2 1.1 convolution_add_fusion.5
  241.2 1.1 convolution_add_fusion.4
  242.3 1.1 convolution_add_fusion.5
  243.4 1.1 convolution_add_fusion.4
  244.5 1.1 convolution_add_fusion.5
  245.5 1.1 convolution_add_fusion.4
  246.6 1.1 convolution_add_fusion.5
  247.7 1.1 convolution_add_fusion.4
  248.8 1.1 convolution_add_fusion.5
  249.9 1.1 convolution_add_fusion.4
  250.9 1.1 convolution_add_fusion.5
  252.0 1.1 convolution_add_fusion.4
  253.1 1.1 convolution_add_fusion.5
  254.2 1.1 convolution_add_fusion.4
  255.2 1.1 convolution_add_fusion.5
  256.3 1.1 convolution_add_fusion.4
  257.4 1.1 convolution_add_fusion.5
  258.5 1.1 convolution_add_fusion.4
  259.6 1.1 convolution_add_fusion.5
  260.6 1.1 convolution_add_fusion.4
  261.7 1.1 convolution_add_fusion.5
  262.8 1.1 convolution_add_fusion.4
  263.9 1.1 convolution_add_fusion.5
  264.9 1.1 convolution_add_fusion.4
  266.0 1.1 convolution_add_fusion.5
  267.1 1.1 convolution_add_fusion.4
  268.2 1.1 convolution_add_fusion.5
  269.3 1.1 convolution_add_fusion.4
  270.3 1.1 convolution_add_fusion.5
  271.4 1.1 convolution_add_fusion.4
  272.5 1.1 convolution_add_fusion.5
  273.6 1.1 convolution_add_fusion.4
  274.6 1.1 convolution_add_fusion.5
  275.7 1.1 convolution_add_fusion.4
  276.8 1.1 convolution_add_fusion.5
  277.9 1.1 convolution_add_fusion.4
  279.0 1.1 convolution_add_fusion.5
  280.0 1.1 convolution_add_fusion.4
  281.1 1.1 convolution_add_fusion.5
  282.2 1.1 convolution_add_fusion.4
  283.3 1.1 convolution_add_fusion.5
  284.3 1.1 convolution_add_fusion.4
  285.4 1.1 convolution_add_fusion.5
  286.5 1.1 convolution_add_fusion.4
  288.7 1.1 convolution_add_fusion.4
  290.8 1.1 convolution_add_fusion.4
  293.0 1.1 convolution_add_fusion.4
  295.1 1.1 convolution_add_fusion.4
  297.3 1.1 convolution_add_fusion.4
  299.4 1.1 convolution_add_fusion.4
  (24 shorter events, 13.6 us)
Async XLA Ops:
  6.5 169.6 %reduce-scatter.2.cloned.1.call-start = ((), (), s32[]{:S(2)}) async-start(), calls=%async_computation.1 | async-start | bytes 3244032 | tf_op jit(solution)/shard_map/reduce_scatter | solution.py:60
  71.2 161.4 %all-gather.2.cloned.1.call-start = ((), (), s32[]{:S(2)}) async-start(), calls=%async_computation.2 | async-start | bytes 1622016 | tf_op jit(solution)/shard_map/all_gather | solution.py:64
  301.6 0.6 copy-start
Sparse Core Ops, SparseCore 0:
  71.3 104.8 reduce-scatter.1
  179.0 53.5 all-gather.1
where the time goes:
time: 311 us; the launch traced here: 309 us
  matrix products  129 us (41%)
  waiting for transfers between devices  124 us (40%)
  other arithmetic  41 us (13%)
  between operations  13.5 us (4%)
    reduce_scatter x1, waiting for transfers between devices, shards(): lax.psum_scatter(terms, ('wide', 'narrow'), scatter_dimension=1, tiled=True)  104 us
    dot_general x32, matrix products, apply_block(): jnp.dot(piece[:half], cosine, preferred_element_type=jnp.float32)  34.5 us
    dot_general x32, matrix products, apply_block(): jnp.dot(piece[half:], sine, preferred_element_type=jnp.float32)  34.5 us
    convert_element_type x1, other arithmetic, make_tables(): jnp.sin(theta).astype(jnp.bfloat16)  34.2 us
    dot_general x1, matrix products, shards(): lax.dot_general(force_bf, sin_table, dims, preferred_element_type=jnp.flo...  30.4 us
    dot_general x1, matrix products, shards(): lax.dot_general(force_bf, cos_table, dims, preferred_element_type=jnp.flo...  29.7 us
    all_gather x1, waiting for transfers between devices, shards(): piece = lax.all_gather(scaled, ('wide', 'narrow'), axis=1, tiled=True)  19.7 us
  transfers between devices with their start and end apart: 2, of which 2 were waited for; matrix products, arithmetic and copies ran while one was open for 11% of the time, Pallas kernels for 0%

commit v1 on v0

--- a/solution.py
+++ b/solution.py
@@ -61,7 +61,12 @@
     cols = owned.shape[1]
     wblock = lax.dynamic_slice_in_dim(waves, lax.axis_index(("wide", "narrow")) * cols, cols, 1)
     scaled = scale_sums(owned, wblock, amp)
-    piece = lax.all_gather(scaled, ("wide", "narrow"), axis=1, tiled=True)
+    piece = jnp.concatenate(
+        lax.all_to_all(
+            jnp.stack([scaled] * lax.axis_size(("wide", "narrow"))), ("wide", "narrow"), 0, 0
+        ),
+        axis=1,
+    )
     cols = piece.shape[1]
 
     def inner(step, acc):

time: 311 us -> 298 us (0.958)
  waiting for transfers between devices: 124 us -> 108 us
  starting transfers between devices: 0.04 us -> 3.71 us
    all_gather x1 -> x0, waiting for transfers between devices: 19.7 us -> none  [shards(): piece = lax.all_gather(scaled, ('wide', 'narrow'), axis=1, tiled=True)]
    all_to_all x0 -> x1, starting transfers between devices: none -> 3.71 us  [shards(): lax.all_to_all(jnp.stack([scaled] * lax.axis_size(('wide', 'narrow'))), (...]
    all_to_all x0 -> x1, waiting for transfers between devices: none -> 3.43 us  [shards(): lax.all_to_all(jnp.stack([scaled] * lax.axis_size(('wide', 'narrow'))), (...]
  transfers between devices with their start and end apart: 2 -> 2, of which waited for: 2 -> 2; matrix products, arithmetic and copies ran while one was open for 11% -> 12% of each run, Pallas kernels for 0% -> 0%
where the time goes in v1:
time: 298 us; the launch traced here: 296 us
  matrix products  128 us (43%)
  waiting for transfers between devices  108 us (36%)
  other arithmetic  40.4 us (14%)
  between operations  13.5 us (5%)
  starting transfers between devices  3.71 us (1%)
  local copies, waits for them, and re-layouts  3.04 us (1%)
    reduce_scatter x1, waiting for transfers between devices, shards(): lax.psum_scatter(terms, ('wide', 'narrow'), scatter_dimension=1, tiled=True)  104 us
    convert_element_type x1, other arithmetic, make_tables(): jnp.sin(theta).astype(jnp.bfloat16)  34.2 us
    dot_general x32, matrix products, apply_block(): jnp.dot(piece[:half], cosine, preferred_element_type=jnp.float32)  34 us
    dot_general x32, matrix products, apply_block(): jnp.dot(piece[half:], sine, preferred_element_type=jnp.float32)  33.9 us
    dot_general x1, matrix products, shards(): lax.dot_general(force_bf, sin_table, dims, preferred_element_type=jnp.flo...  30.4 us
    dot_general x1, matrix products, shards(): lax.dot_general(force_bf, cos_table, dims, preferred_element_type=jnp.flo...  29.7 us
  transfers between devices with their start and end apart: 2, of which 2 were waited for; matrix products, arithmetic and copies ran while one was open for 12% of the time, Pallas kernels for 0%

profile of v1, /device:TPU:0, one launch (start us, length us, event | category | flops | bytes accessed | tf_op | source)
XLA Modules:
  0.0 296.4 jit_solution(6948155403430265434)
XLA Ops:
  9.2 29.7 %convolution_bitcast_fusion.1 = f32[48,8192]{1,0:T(8,128)S(1)} fusion(bf16[48,256]{1,0:T(8,128)(2,1)S(1)} %bitcast.40, f32[256]{0:T(256)S(1)} %bitcast.45, f32[8192]{0:T(1024)S(1)} %bitcast.34, f32[256]{0:T(256)S(1)} %bitcast.48, f32[8192]{0:T(1024)S(1)} %bitcast.37, f32[256]{0:T(256)S(1)} %bitcast.42, f32[8192]{0:T(1024)S(1)} %bitcast.31), kind=kOutput, calls=%fused_computation.9 | convolution fusion | flops 216006656 | bytes 1698816 | tf_op jit(solution)/shard_map/dot_general | solution.py:48
  38.9 30.4 %convolution_bitcast_fusion = f32[48,8192]{1,0:T(8,128)S(1)} fusion(bf16[48,256]{1,0:T(8,128)(2,1)S(1)} %bitcast.41, f32[256]{0:T(256)S(1)} %bitcast.46, f32[8192]{0:T(1024)S(1)} %bitcast.35, f32[256]{0:T(256)S(1)} %bitcast.49, f32[8192]{0:T(1024)S(1)} %bitcast.38, f32[256]{0:T(256)S(1)} %bitcast.43, f32[8192]{0:T(1024)S(1)} %bitcast.32), kind=kOutput, calls=%fused_computation.8 | convolution fusion | flops 216006656 | bytes 1698816 | tf_op jit(solution)/shard_map/dot_general | solution.py:49
  69.3 1.9 pad_maximum_fusion
  71.9 104.3 %reduce-scatter.2.cloned.1.call-done = f32[96,256]{1,0:T(8,128)} async-done(((f32[96,8192]{1,0:T(8,128)}), f32[96,256]{1,0:T(8,128)}) %reduce-scatter.2.cloned.1.call-update) | async-done | bytes 98320 | tf_op jit(solution)/shard_map/reduce_scatter | solution.py:60
  178.1 1.4 stack.2
  179.5 3.7 %all-to-all-start = ((bf16[32,96,256]{2,1,0:T(8,128)(2,1)}), bf16[32,96,256]{2,1,0:T(8,128)(2,1)S(1)}, u32[]{:S(2)}, u32[]{:S(2)}) async-start(bf16[32,96,256]{2,1,0:T(8,128)(2,1)} %stack.2), calls=%async_computation.1 | async-start | bytes 3145728 | tf_op jit(solution)/shard_map/all_to_all | solution.py:65
  183.2 34.2 %sine_convert_fusion = (bf16[8192,256]{1,0:T(8,128)(2,1)}, bf16[8192,256]{1,0:T(8,128)(2,1)}) fusion(f32[256]{0:T(256)S(1)} %bitcast.47, f32[8192]{0:T(1024)S(1)} %bitcast.36, f32[256]{0:T(256)S(1)} %bitcast.50, f32[8192]{0:T(1024)S(1)} %bitcast.39, f32[256]{0:T(256)S(1)} %bitcast.44, f32[8192]{0:T(1024)S(1)} %bitcast.33), kind=kLoop, calls=%fused_computation.10 | loop fusion | flops 16777216 | bytes 8489984 | tf_op jit(solution)/shard_map/convert_element_type | solution.py:18
  217.4 3.4 %all-to-all-done = bf16[32,96,256]{2,1,0:T(8,128)(2,1)S(1)} async-done(((bf16[32,96,256]{2,1,0:T(8,128)(2,1)}), bf16[32,96,256]{2,1,0:T(8,128)(2,1)S(1)}, u32[]{:S(2)}, u32[]{:S(2)}) %all-to-all-start) | async-done | bytes 1572896 | tf_op jit(solution)/shard_map/all_to_all | solution.py:65
  221.0 67.9 %while.14 = (s32[]{:T(128)}, f32[48,256]{1,0:T(8,128)S(1)}, bf16[96,8192]{1,0:T(8,128)(2,1)S(1)}, bf16[8192,256]{1,0:T(8,128)(2,1)}, bf16[8192,256]{1,0:T(8,128)...) while((s32[]{:T(128)}, f32[48,256]{1,0:T(8,128)S(1)}, ...), condition=%wide.region_4.0_spmd.clone, body=%wide.region_3.0_spmd.clone.sunk | while | flops 12619784 | bytes 511144 | solution.py:76
  223.1 1.1 convolution_add_fusion.4
  224.1 1.1 convolution_add_fusion.5
  225.2 1.1 convolution_add_fusion.4
  226.3 1.1 convolution_add_fusion.5
  227.3 1.1 convolution_add_fusion.4
  228.4 1.1 convolution_add_fusion.5
  229.5 1.1 convolution_add_fusion.4
  231.6 1.1 convolution_add_fusion.4
  232.6 1.1 convolution_add_fusion.5
  233.7 1.1 convolution_add_fusion.4
  234.8 1.1 convolution_add_fusion.5
  235.8 1.1 convolution_add_fusion.4
  236.9 1.1 convolution_add_fusion.5
  237.9 1.1 convolution_add_fusion.4
  240.1 1.1 convolution_add_fusion.4
  241.1 1.1 convolution_add_fusion.5
  242.2 1.1 convolution_add_fusion.4
  243.2 1.1 convolution_add_fusion.5
  244.3 1.1 convolution_add_fusion.4
  245.4 1.1 convolution_add_fusion.5
  246.4 1.1 convolution_add_fusion.4
  248.6 1.1 convolution_add_fusion.4
  249.6 1.1 convolution_add_fusion.5
  250.7 1.1 convolution_add_fusion.4
  251.7 1.1 convolution_add_fusion.5
  252.8 1.1 convolution_add_fusion.4
  253.9 1.1 convolution_add_fusion.5
  254.9 1.1 convolution_add_fusion.4
  257.0 1.1 convolution_add_fusion.4
  258.1 1.1 convolution_add_fusion.5
  259.2 1.1 convolution_add_fusion.4
  260.2 1.1 convolution_add_fusion.5
  261.3 1.1 convolution_add_fusion.4
  262.3 1.1 convolution_add_fusion.5
  263.4 1.1 convolution_add_fusion.4
  265.5 1.1 convolution_add_fusion.4
  266.6 1.1 convolution_add_fusion.5
  267.6 1.1 convolution_add_fusion.4
  268.7 1.1 convolution_add_fusion.5
  269.8 1.1 convolution_add_fusion.4
  270.8 1.1 convolution_add_fusion.5
  271.9 1.1 convolution_add_fusion.4
  274.0 1.1 convolution_add_fusion.4
  275.1 1.1 convolution_add_fusion.5
  276.1 1.1 convolution_add_fusion.4
  277.2 1.1 convolution_add_fusion.5
  278.3 1.1 convolution_add_fusion.4
  279.3 1.1 convolution_add_fusion.5
  280.4 1.1 convolution_add_fusion.4
  282.5 1.1 convolution_add_fusion.4
  283.6 1.1 convolution_add_fusion.5
  284.6 1.1 convolution_add_fusion.4
  285.7 1.1 convolution_add_fusion.5
  286.8 1.1 convolution_add_fusion.4
  287.8 1.1 convolution_add_fusion.5
  (25 shorter events, 15.4 us)
Async XLA Ops:
  6.5 169.7 %reduce-scatter.2.cloned.1.call-start = ((), (), s32[]{:S(2)}) async-start(), calls=%async_computation.2 | async-start | bytes 3244032 | tf_op jit(solution)/shard_map/reduce_scatter | solution.py:60
  179.5 41.4 %all-to-all-start = ((bf16[32,96,256]{2,1,0:T(8,128)(2,1)}), bf16[32,96,256]{2,1,0:T(8,128)(2,1)S(1)}, u32[]{:S(2)}, u32[]{:S(2)}) async-start(bf16[32,96,256]{2,1,0:T(8,128)(2,1)} %stack.2), calls=%async_computation.1 | async-start | bytes 3145728 | tf_op jit(solution)/shard_map/all_to_all | solution.py:65
  288.9 0.6 copy-start
Sparse Core Ops, SparseCore 0:
  71.3 104.8 reduce-scatter.1
